TPU v7x, 256 devices: a whole 4x4x8 slice. The times are simulated.
256 devices in a mesh: gx: 64 (over y, z, core), gy: 4 (over x).
Axes of the slice: x: 4, y: 4, z: 8, core: 2. Of those that a mesh axis runs over, the one named last changes fastest.
Arguments:
- members_state: float32 [3, 64, 512, 512], P(None, None, 'gx', 'gy'), may hold values from -6 to 6
- depth_level: int32 [512, 512], P('gx', 'gy'), may hold values from 1 to 8
- land_mask: int32 [512, 512], P('gx', 'gy'), may hold values 0 or 1
- obs_cells: int32 [64, 4, 256], P('gx', 'gy'), may hold values from 0 to 1023
- obs_values: float32 [64, 4, 256], P('gx', 'gy'), may hold values from -6 to 6
- obs_error: float32 [64, 4, 256], P('gx', 'gy'), may hold values from 2 to 8
Outputs:
- analysis: float32 [3, 64, 512, 512], P(None, None, 'gx', 'gy')
Inputs may be any that keep to these rules, and one draw needn't show every extreme that they name: Each value of obs_cells is the row-major index of a cell within the 8 x 128 block held by the device at the same position along gx and gy.
All inputs are finite; a program needn't handle non-finite values. No bound on the sum of `land_mask` on one device may be relied on, other than what follows from the above.
Results may differ from a plain program's by a relative error of at most 0.00005.
Values sent between devices are 32-bit elements; how exact they have to be, the bound alone decides.
No kernel may reach another device: no remote copies, remote signals or barrier semaphores. Data moves between devices by JAX's collectives and lax.ppermute only.
A program may use at most 64 MiB of HBM per device.

v0:
```python
import jax
import jax.numpy as jnp
from jax import lax
from jax.sharding import PartitionSpec as P


def extended(block, sides, width):
    for axis, dim in sides:
        count = lax.axis_size(axis)
        forward = [(i, i + 1) for i in range(count - 1)]
        backward = [(target, source) for source, target in forward]
        low = lax.ppermute(
            lax.slice_in_dim(block, block.shape[dim] - width, None, axis=dim), axis, forward
        )
        high = lax.ppermute(lax.slice_in_dim(block, 0, width, axis=dim), axis, backward)
        block = jnp.concatenate([low, block, high], axis=dim)
    return block


def height_tendency(padded, geo):
    h = padded[0]
    u = padded[1]
    v = padded[2]
    depth = geo[0]
    mask = geo[1][1:-1, 1:-1]
    east = depth * u
    north = depth * v

    def along_x(a):
        return (a[:, 2:, 1:-1] - a[:, :-2, 1:-1]) * 0.5

    def along_y(a):
        return (a[:, 1:-1, 2:] - a[:, 1:-1, :-2]) * 0.5

    def laplace(a):
        return (
            a[:, 2:, 1:-1]
            + a[:, :-2, 1:-1]
            + a[:, 1:-1, 2:]
            + a[:, 1:-1, :-2]
            - 4.0 * a[:, 1:-1, 1:-1]
        )

    def inner(a):
        return a[:, 1:-1, 1:-1]

    dh = -along_x(east) - along_y(north) + 0.05 * laplace(h)
    du = -along_x(h) + 0.2 * inner(v) + 0.05 * laplace(u)
    dv = -along_y(h) - 0.2 * inner(u) + 0.05 * laplace(v)
    return jnp.stack([dh, du, dv]) * mask


def tri_solve(lower, rhs, flipped):
    return lax.linalg.triangular_solve(lower, rhs, left_side=True, lower=True, transpose_a=flipped)


def padded_section(field):
    return extended(field, (("gx", 2), ("gy", 3)), 1)


def local(members_state, depth_level, land_mask, obs_cells, obs_values, obs_error):
    maskf = land_mask.astype(jnp.float32)
    geo = jnp.stack([0.25 * depth_level.astype(jnp.float32) * maskf, maskf])
    geo_wide = extended(geo, (("gx", 1), ("gy", 2)), 3)
    first_offset = members_state * maskf
    single_geometry = geo_wide[:, 2:-2, 2:-2]
    s1 = first_offset + 0.3 * height_tendency(padded_section(first_offset), single_geometry)
    variance_estimate2 = 0.75 * first_offset + 0.25 * (
        s1 + 0.3 * height_tendency(padded_section(s1), single_geometry)
    )
    prior_model_vector = 1.0 / 3.0 * first_offset + 2.0 / 3.0 * (
        variance_estimate2
        + 0.3 * height_tendency(padded_section(variance_estimate2), single_geometry)
    )
    sample_average = jnp.mean(prior_model_vector, axis=1, keepdims=True)
    sample_deviations = prior_model_vector - sample_average
    sample_number = prior_model_vector.shape[1]
    free_elevation_field = prior_model_vector[0].reshape(sample_number, -1)
    measured_data = jnp.take(free_elevation_field, obs_cells.reshape(-1), axis=1)
    obs_mean = jnp.mean(measured_data, axis=0, keepdims=True)
    error = obs_error.reshape(-1)
    scaled = (measured_data - obs_mean) / (error * jnp.sqrt(jnp.float32(sample_number - 1)))
    innovation = (obs_values.reshape(-1) - obs_mean[0]) / error
    gram_part = jnp.dot(scaled, scaled.T, precision=lax.Precision.HIGHEST)
    proj_part = jnp.dot(scaled, innovation, precision=lax.Precision.HIGHEST)
    eye = jnp.eye(sample_number, dtype=jnp.float32)
    gram, projection = lax.psum((gram_part, proj_part), ("gx", "gy"))
    lower = jnp.linalg.cholesky(eye + gram)
    half = tri_solve(lower, projection[:, None], False)
    weights = tri_solve(lower, half, True)[:, 0]
    inverse = tri_solve(lower, eye, False)
    transform = weights[:, None] / jnp.sqrt(jnp.float32(sample_number - 1)) + inverse.T
    mixed = jnp.einsum(
        "km,fkxy->fmxy", transform, sample_deviations, precision=lax.Precision.HIGHEST
    )
    return sample_average + mixed


def solution(mesh):
    placed = (
        P(None, None, "gx", "gy"),
        P("gx", "gy"),
        P("gx", "gy"),
        P("gx", "gy", None),
        P("gx", "gy", None),
        P("gx", "gy", None),
    )
    return jax.shard_map(
        local, mesh=mesh, in_specs=placed, out_specs=P(None, None, "gx", "gy"), check_vma=False
    )
```

profile of v0, /device:TPU:1, one launch (start us, length us, event | category | flops | bytes accessed | tf_op | source)
XLA Modules:
  0.0 180.3 jit_solution(6452280479091019301)
XLA Ops:
  1.4 5.1 %collective-permute-start.1 = (f32[2,3,128]{2,1,0:T(4,128)S(1)}, f32[2,3,128]{2,1,0:T(4,128)S(1)}, u32[]{:S(2)}, u32[]{:S(2)}) collective-permute-start(f32[2,3,128]{2,1,0:T(4,128)S(1)} %get-tuple-element.47), channel_id=1, source_target_pairs={{4,0},{8,4},{12,8},{16,12},{20,16},{24,20},{28,24},{32,28},{36,32}... | collective-permute-start | bytes 9224 | tf_op jit(solution)/shard_map/ppermute | solution.py:15
  6.5 1.9 %collective-permute-start = (f32[2,3,128]{2,1,0:T(4,128)S(1)}, f32[2,3,128]{2,1,0:T(4,128)S(1)}, u32[]{:S(2)}, u32[]{:S(2)}) collective-permute-start(f32[2,3,128]{2,1,0:T(4,128)S(1)} %get-tuple-element.46), channel_id=1, source_target_pairs={{0,4},{4,8},{8,12},{12,16},{16,20},{20,24},{24,28},{28,32},{32,36}... | collective-permute-start | bytes 9224 | tf_op jit(solution)/shard_map/ppermute | solution.py:12
  8.4 1.6 copy.15
  11.7 4.0 %collective-permute-start.2 = (f32[2,14,3]{2,1,0:T(8,128)S(1)}, f32[2,14,3]{2,1,0:T(8,128)S(1)}, u32[]{:S(2)}, u32[]{:S(2)}) collective-permute-start(f32[2,14,3]{2,1,0:T(8,128)S(1)} %get-tuple-element.44), channel_id=1, source_target_pairs={{0,1},{1,2},{2,3},{4,5},{5,6},{6,7},{8,9},{9,10},{10,11},{12,13},{... | collective-permute-start | bytes 1016 | tf_op jit(solution)/shard_map/ppermute | solution.py:12
  15.7 3.0 %collective-permute-start.5 = (f32[3,64,1,128]{1,3,2,0:T(8,128)S(1)}, f32[3,64,1,128]{1,3,2,0:T(8,128)S(1)}, u32[]{:S(2)}, u32[]{:S(2)}) collective-permute-start(f32[3,64,1,128]{1,3,2,0:T(8,128)S(1)} %get-tuple-element.41), channel_id=1, source_target_pairs={{4,0},{8,4},{12,8},{16,12},{20,16},{24,20},{28,24},{32,28},{36,32}... | collective-permute-start | bytes 294920 | tf_op jit(solution)/shard_map/ppermute | solution.py:15
  18.7 2.6 %collective-permute-start.4 = (f32[3,64,1,128]{1,3,2,0:T(8,128)S(1)}, f32[3,64,1,128]{1,3,2,0:T(8,128)S(1)}, u32[]{:S(2)}, u32[]{:S(2)}) collective-permute-start(f32[3,64,1,128]{1,3,2,0:T(8,128)S(1)} %get-tuple-element.40), channel_id=1, source_target_pairs={{0,4},{4,8},{8,12},{12,16},{16,20},{20,24},{24,28},{28,32},{32,36}... | collective-permute-start | bytes 294920 | tf_op jit(solution)/shard_map/ppermute | solution.py:12
  21.4 1.3 collective-permute-done.5
  23.9 1.3 collective-permute-start.7
  25.2 4.0 %collective-permute-start.6 = (f32[3,64,10,1]{1,3,2,0:T(1,128)S(1)}, f32[3,64,10,1]{1,3,2,0:T(1,128)S(1)}, u32[]{:S(2)}, u32[]{:S(2)}) collective-permute-start(f32[3,64,10,1]{1,3,2,0:T(1,128)S(1)} %get-tuple-element.34), channel_id=1, source_target_pairs={{0,1},{1,2},{2,3},{4,5},{5,6},{6,7},{8,9},{9,10},{10,11},{12,13},{... | collective-permute-start | bytes 23048 | tf_op jit(solution)/shard_map/ppermute | solution.py:12
  32.1 1.9 %collective-permute-start.9 = (f32[3,64,1,128]{1,3,2,0:T(8,128)S(1)}, f32[3,64,1,128]{1,3,2,0:T(8,128)S(1)}, u32[]{:S(2)}, u32[]{:S(2)}) collective-permute-start(f32[3,64,1,128]{1,3,2,0:T(8,128)S(1)} %get-tuple-element.39), channel_id=1, source_target_pairs={{4,0},{8,4},{12,8},{16,12},{20,16},{24,20},{28,24},{32,28},{36,32}... | collective-permute-start | bytes 294920 | tf_op jit(solution)/shard_map/ppermute | solution.py:15
  34.1 5.5 %collective-permute-start.8 = (f32[3,64,1,128]{1,3,2,0:T(8,128)S(1)}, f32[3,64,1,128]{1,3,2,0:T(8,128)S(1)}, u32[]{:S(2)}, u32[]{:S(2)}) collective-permute-start(f32[3,64,1,128]{1,3,2,0:T(8,128)S(1)} %get-tuple-element.38), channel_id=1, source_target_pairs={{0,4},{4,8},{8,12},{12,16},{16,20},{20,24},{24,28},{28,32},{32,36}... | collective-permute-start | bytes 294920 | tf_op jit(solution)/shard_map/ppermute | solution.py:12
  39.6 1.4 collective-permute-done.9
  42.2 1.3 collective-permute-start.11
  43.5 4.5 %collective-permute-start.10 = (f32[3,64,10,1]{1,3,2,0:T(1,128)S(1)}, f32[3,64,10,1]{1,3,2,0:T(1,128)S(1)}, u32[]{:S(2)}, u32[]{:S(2)}) collective-permute-start(f32[3,64,10,1]{1,3,2,0:T(1,128)S(1)} %get-tuple-element.32), channel_id=1, source_target_pairs={{0,1},{1,2},{2,3},{4,5},{5,6},{6,7},{8,9},{9,10},{10,11},{12,13},{... | collective-permute-start | bytes 23048 | tf_op jit(solution)/shard_map/ppermute | solution.py:12
  51.4 1.9 %collective-permute-start.13 = (f32[3,64,1,128]{1,3,2,0:T(8,128)S(1)}, f32[3,64,1,128]{1,3,2,0:T(8,128)S(1)}, u32[]{:S(2)}, u32[]{:S(2)}) collective-permute-start(f32[3,64,1,128]{1,3,2,0:T(8,128)S(1)} %get-tuple-element.37), channel_id=1, source_target_pairs={{4,0},{8,4},{12,8},{16,12},{20,16},{24,20},{28,24},{32,28},{36,32}... | collective-permute-start | bytes 294920 | tf_op jit(solution)/shard_map/ppermute | solution.py:15
  53.3 5.2 %collective-permute-start.12 = (f32[3,64,1,128]{1,3,2,0:T(8,128)S(1)}, f32[3,64,1,128]{1,3,2,0:T(8,128)S(1)}, u32[]{:S(2)}, u32[]{:S(2)}) collective-permute-start(f32[3,64,1,128]{1,3,2,0:T(8,128)S(1)} %get-tuple-element.36), channel_id=1, source_target_pairs={{0,4},{4,8},{8,12},{12,16},{16,20},{20,24},{24,28},{28,32},{32,36}... | collective-permute-start | bytes 294920 | tf_op jit(solution)/shard_map/ppermute | solution.py:12
  58.6 1.4 collective-permute-done.13
  62.5 4.5 %collective-permute-start.14 = (f32[3,64,10,1]{1,3,2,0:T(1,128)S(1)}, f32[3,64,10,1]{1,3,2,0:T(1,128)S(1)}, u32[]{:S(2)}, u32[]{:S(2)}) collective-permute-start(f32[3,64,10,1]{1,3,2,0:T(1,128)S(1)} %get-tuple-element.30), channel_id=1, source_target_pairs={{0,1},{1,2},{2,3},{4,5},{5,6},{6,7},{8,9},{9,10},{10,11},{12,13},{... | collective-permute-start | bytes 23048 | tf_op jit(solution)/shard_map/ppermute | solution.py:12
  69.5 1.7 fusion.77
  73.0 91.1 %all-reduce = (f32[64,64]{1,0:T(8,128)S(1)}, f32[64]{0:T(128)S(1)}) all-reduce(f32[64,64]{1,0:T(8,128)S(1)} %fusion.83, f32[64]{0:T(128)S(1)} %convolution_bitcast_fusion.2), channel_id=1, replica_groups=mesh['gx'=64,'gy'=4] {'gx','gy'}, use_global_device_ids=true, to_apply=%region_2.3 | all-reduce | flops 4160 | bytes 33280 | tf_op jit(solution)/shard_map/psum | solution.py:87
  164.2 5.8 %cholesky.18 = f32[64,64]{1,0:T(8,128)S(1)} custom-call(f32[64,64]{1,0:T(8,128)S(1)} %fusion.74), custom_call_target="Cholesky" | custom-call | tf_op jit(solution)/shard_map/jit(cholesky)/cholesky | solution.py:88
  171.4 4.9 %custom-call.10 = f32[1,64,64]{1,2,0:T(8,128)S(1)} custom-call(f32[1,64,64]{2,1,0:T(8,128)S(1)} %fusion.70), custom_call_target="InvertDiagBlocksLowerTriangular" | custom-call | tf_op jit(solution)/shard_map/triangular_solve | solution.py:54
  176.9 2.1 %fusion.15 = f32[3,64,8,128]{3,1,2,0:T(8,128)S(1)} fusion(f32[64,64,1,1]{1,0,3,2:T(8,128)S(1)} %fusion.18, f32[3,64,8,128]{1,3,2,0:T(8,128)S(1)} %get-tuple-element.8, f32[3,8,128]{2,1,0:T(8,128)S(1)} %broadcast_multiply_fusion.7), kind=kOutput, calls=%fused_computation.20 | convolution fusion | flops 151388160 | bytes 1601536 | tf_op jit(solution)/shard_map/km,fkxy->fmxy/dot_general | solution.py:93
  179.0 1.3 copy.19
  (73 shorter events, 20.3 us)
Async XLA Ops:
  1.4 8.9 %collective-permute-start.1 = (f32[2,3,128]{2,1,0:T(4,128)S(1)}, f32[2,3,128]{2,1,0:T(4,128)S(1)}, u32[]{:S(2)}, u32[]{:S(2)}) collective-permute-start(f32[2,3,128]{2,1,0:T(4,128)S(1)} %get-tuple-element.47), channel_id=1, source_target_pairs={{4,0},{8,4},{12,8},{16,12},{20,16},{24,20},{28,24},{32,28},{36,32}... | collective-permute-start | bytes 9224 | tf_op jit(solution)/shard_map/ppermute | solution.py:15
  6.5 3.8 %collective-permute-start = (f32[2,3,128]{2,1,0:T(4,128)S(1)}, f32[2,3,128]{2,1,0:T(4,128)S(1)}, u32[]{:S(2)}, u32[]{:S(2)}) collective-permute-start(f32[2,3,128]{2,1,0:T(4,128)S(1)} %get-tuple-element.46), channel_id=1, source_target_pairs={{0,4},{4,8},{8,12},{12,16},{16,20},{20,24},{24,28},{28,32},{32,36}... | collective-permute-start | bytes 9224 | tf_op jit(solution)/shard_map/ppermute | solution.py:12
  10.4 10.9 %collective-permute-start.3 = (f32[2,14,3]{2,1,0:T(8,128)S(1)}, f32[2,14,3]{2,1,0:T(8,128)S(1)}, u32[]{:S(2)}, u32[]{:S(2)}) collective-permute-start(f32[2,14,3]{2,1,0:T(8,128)S(1)} %get-tuple-element.45), channel_id=1, source_target_pairs={{1,0},{2,1},{3,2},{5,4},{6,5},{7,6},{9,8},{10,9},{11,10},{13,12},{... | collective-permute-start | bytes 1016 | tf_op jit(solution)/shard_map/ppermute | solution.py:15
  11.7 9.6 %collective-permute-start.2 = (f32[2,14,3]{2,1,0:T(8,128)S(1)}, f32[2,14,3]{2,1,0:T(8,128)S(1)}, u32[]{:S(2)}, u32[]{:S(2)}) collective-permute-start(f32[2,14,3]{2,1,0:T(8,128)S(1)} %get-tuple-element.44), channel_id=1, source_target_pairs={{0,1},{1,2},{2,3},{4,5},{5,6},{6,7},{8,9},{9,10},{10,11},{12,13},{... | collective-permute-start | bytes 1016 | tf_op jit(solution)/shard_map/ppermute | solution.py:12
  15.7 7.0 %collective-permute-start.5 = (f32[3,64,1,128]{1,3,2,0:T(8,128)S(1)}, f32[3,64,1,128]{1,3,2,0:T(8,128)S(1)}, u32[]{:S(2)}, u32[]{:S(2)}) collective-permute-start(f32[3,64,1,128]{1,3,2,0:T(8,128)S(1)} %get-tuple-element.41), channel_id=1, source_target_pairs={{4,0},{8,4},{12,8},{16,12},{20,16},{24,20},{28,24},{32,28},{36,32}... | collective-permute-start | bytes 294920 | tf_op jit(solution)/shard_map/ppermute | solution.py:15
  18.7 5.2 %collective-permute-start.4 = (f32[3,64,1,128]{1,3,2,0:T(8,128)S(1)}, f32[3,64,1,128]{1,3,2,0:T(8,128)S(1)}, u32[]{:S(2)}, u32[]{:S(2)}) collective-permute-start(f32[3,64,1,128]{1,3,2,0:T(8,128)S(1)} %get-tuple-element.40), channel_id=1, source_target_pairs={{0,4},{4,8},{8,12},{12,16},{16,20},{20,24},{24,28},{28,32},{32,36}... | collective-permute-start | bytes 294920 | tf_op jit(solution)/shard_map/ppermute | solution.py:12
  23.9 5.5 %collective-permute-start.7 = (f32[3,64,10,1]{1,3,2,0:T(1,128)S(1)}, f32[3,64,10,1]{1,3,2,0:T(1,128)S(1)}, u32[]{:S(2)}, u32[]{:S(2)}) collective-permute-start(f32[3,64,10,1]{1,3,2,0:T(1,128)S(1)} %get-tuple-element.35), channel_id=1, source_target_pairs={{1,0},{2,1},{3,2},{5,4},{6,5},{7,6},{9,8},{10,9},{11,10},{13,12},{... | collective-permute-start | bytes 23048 | tf_op jit(solution)/shard_map/ppermute | solution.py:15
  25.2 4.8 %collective-permute-start.6 = (f32[3,64,10,1]{1,3,2,0:T(1,128)S(1)}, f32[3,64,10,1]{1,3,2,0:T(1,128)S(1)}, u32[]{:S(2)}, u32[]{:S(2)}) collective-permute-start(f32[3,64,10,1]{1,3,2,0:T(1,128)S(1)} %get-tuple-element.34), channel_id=1, source_target_pairs={{0,1},{1,2},{2,3},{4,5},{5,6},{6,7},{8,9},{9,10},{10,11},{12,13},{... | collective-permute-start | bytes 23048 | tf_op jit(solution)/shard_map/ppermute | solution.py:12
  32.1 16.0 %copy-start = (s32[1,1,256]{2,1,0:T(1,128)S(1)}, s32[1,1,256]{2,1,0:T(1,128)}, u32[]{:S(2)}) copy-start(s32[1,1,256]{2,1,0:T(1,128)} %param.9) | copy-start | bytes 3076
  32.1 8.9 %collective-permute-start.9 = (f32[3,64,1,128]{1,3,2,0:T(8,128)S(1)}, f32[3,64,1,128]{1,3,2,0:T(8,128)S(1)}, u32[]{:S(2)}, u32[]{:S(2)}) collective-permute-start(f32[3,64,1,128]{1,3,2,0:T(8,128)S(1)} %get-tuple-element.39), channel_id=1, source_target_pairs={{4,0},{8,4},{12,8},{16,12},{20,16},{24,20},{28,24},{32,28},{36,32}... | collective-permute-start | bytes 294920 | tf_op jit(solution)/shard_map/ppermute | solution.py:15
  34.1 8.1 %collective-permute-start.8 = (f32[3,64,1,128]{1,3,2,0:T(8,128)S(1)}, f32[3,64,1,128]{1,3,2,0:T(8,128)S(1)}, u32[]{:S(2)}, u32[]{:S(2)}) collective-permute-start(f32[3,64,1,128]{1,3,2,0:T(8,128)S(1)} %get-tuple-element.38), channel_id=1, source_target_pairs={{0,4},{4,8},{8,12},{12,16},{16,20},{20,24},{24,28},{28,32},{32,36}... | collective-permute-start | bytes 294920 | tf_op jit(solution)/shard_map/ppermute | solution.py:12
  42.2 5.9 %collective-permute-start.11 = (f32[3,64,10,1]{1,3,2,0:T(1,128)S(1)}, f32[3,64,10,1]{1,3,2,0:T(1,128)S(1)}, u32[]{:S(2)}, u32[]{:S(2)}) collective-permute-start(f32[3,64,10,1]{1,3,2,0:T(1,128)S(1)} %get-tuple-element.33), channel_id=1, source_target_pairs={{1,0},{2,1},{3,2},{5,4},{6,5},{7,6},{9,8},{10,9},{11,10},{13,12},{... | collective-permute-start | bytes 23048 | tf_op jit(solution)/shard_map/ppermute | solution.py:15
  43.5 5.4 %collective-permute-start.10 = (f32[3,64,10,1]{1,3,2,0:T(1,128)S(1)}, f32[3,64,10,1]{1,3,2,0:T(1,128)S(1)}, u32[]{:S(2)}, u32[]{:S(2)}) collective-permute-start(f32[3,64,10,1]{1,3,2,0:T(1,128)S(1)} %get-tuple-element.32), channel_id=1, source_target_pairs={{0,1},{1,2},{2,3},{4,5},{5,6},{6,7},{8,9},{9,10},{10,11},{12,13},{... | collective-permute-start | bytes 23048 | tf_op jit(solution)/shard_map/ppermute | solution.py:12
  51.4 8.6 %collective-permute-start.13 = (f32[3,64,1,128]{1,3,2,0:T(8,128)S(1)}, f32[3,64,1,128]{1,3,2,0:T(8,128)S(1)}, u32[]{:S(2)}, u32[]{:S(2)}) collective-permute-start(f32[3,64,1,128]{1,3,2,0:T(8,128)S(1)} %get-tuple-element.37), channel_id=1, source_target_pairs={{4,0},{8,4},{12,8},{16,12},{20,16},{24,20},{28,24},{32,28},{36,32}... | collective-permute-start | bytes 294920 | tf_op jit(solution)/shard_map/ppermute | solution.py:15
  53.3 7.8 %collective-permute-start.12 = (f32[3,64,1,128]{1,3,2,0:T(8,128)S(1)}, f32[3,64,1,128]{1,3,2,0:T(8,128)S(1)}, u32[]{:S(2)}, u32[]{:S(2)}) collective-permute-start(f32[3,64,1,128]{1,3,2,0:T(8,128)S(1)} %get-tuple-element.36), channel_id=1, source_target_pairs={{0,4},{4,8},{8,12},{12,16},{16,20},{20,24},{24,28},{28,32},{32,36}... | collective-permute-start | bytes 294920 | tf_op jit(solution)/shard_map/ppermute | solution.py:12
  61.2 5.9 %collective-permute-start.15 = (f32[3,64,10,1]{1,3,2,0:T(1,128)S(1)}, f32[3,64,10,1]{1,3,2,0:T(1,128)S(1)}, u32[]{:S(2)}, u32[]{:S(2)}) collective-permute-start(f32[3,64,10,1]{1,3,2,0:T(1,128)S(1)} %get-tuple-element.31), channel_id=1, source_target_pairs={{1,0},{2,1},{3,2},{5,4},{6,5},{7,6},{9,8},{10,9},{11,10},{13,12},{... | collective-permute-start | bytes 23048 | tf_op jit(solution)/shard_map/ppermute | solution.py:15
  62.5 5.4 %collective-permute-start.14 = (f32[3,64,10,1]{1,3,2,0:T(1,128)S(1)}, f32[3,64,10,1]{1,3,2,0:T(1,128)S(1)}, u32[]{:S(2)}, u32[]{:S(2)}) collective-permute-start(f32[3,64,10,1]{1,3,2,0:T(1,128)S(1)} %get-tuple-element.30), channel_id=1, source_target_pairs={{0,1},{1,2},{2,3},{4,5},{5,6},{6,7},{8,9},{9,10},{10,11},{12,13},{... | collective-permute-start | bytes 23048 | tf_op jit(solution)/shard_map/ppermute | solution.py:12
  71.3 1.0 copy-start.1
  71.3 1.0 copy-start.2
where the time goes:
time: 181 us; the launch traced here: 180 us
  blocking collectives  91.1 us (50%)
  starting transfers between devices  49.4 us (27%)
  other arithmetic  21.6 us (12%)
  waiting for transfers between devices  9.98 us (6%)
  local copies, waits for them, and re-layouts  4.53 us (3%)
  matrix products  3.22 us (2%)
    psum x1, blocking collectives, local(): gram, projection = lax.psum((gram_part, proj_part), ('gx', 'gy'))  91.1 us
    ppermute x8, starting transfers between devices, extended(): lax.ppermute(lax.slice_in_dim(block, block.shape[dim] - width, None, axis...  32.4 us
    ppermute x8, starting transfers between devices, extended(): lax.ppermute(lax.slice_in_dim(block, 0, width, axis=dim), axis, backward)  17.1 us
    another operation x3, other arithmetic, local(): lower = jnp.linalg.cholesky(eye + gram)  6.52 us
    ppermute x8, waiting for transfers between devices, extended(): lax.ppermute(lax.slice_in_dim(block, block.shape[dim] - width, None, axis...  5.86 us
    another operation x2, other arithmetic, tri_solve(): lax.linalg.triangular_solve(lower, rhs, left_side=True, lower=True, trans...  5.55 us
    ppermute x8, waiting for transfers between devices, extended(): lax.ppermute(lax.slice_in_dim(block, 0, width, axis=dim), axis, backward)  4.11 us
  transfers between devices with their start and end apart: 16, of which 9 were waited for; matrix products, arithmetic and copies ran while one was open for 1% of the time, Pallas kernels for 0%

commit v1 on v0

--- a/solution.py
+++ b/solution.py
@@ -2,6 +2,11 @@
 import jax.numpy as jnp
 from jax import lax
 from jax.sharding import PartitionSpec as P
+
+
+def by_each_axis(value, inner_axis, outer_axis):
+    middle = lax.psum(value, inner_axis)
+    return lax.psum(middle, outer_axis)
 
 
 def extended(block, sides, width):
@@ -84,7 +89,7 @@
     gram_part = jnp.dot(scaled, scaled.T, precision=lax.Precision.HIGHEST)
     proj_part = jnp.dot(scaled, innovation, precision=lax.Precision.HIGHEST)
     eye = jnp.eye(sample_number, dtype=jnp.float32)
-    gram, projection = lax.psum((gram_part, proj_part), ("gx", "gy"))
+    gram, projection = by_each_axis((gram_part, proj_part), "gx", "gy")
     lower = jnp.linalg.cholesky(eye + gram)
     half = tri_solve(lower, projection[:, None], False)
     weights = tri_solve(lower, half, True)[:, 0]

time: 181 us -> 358 us (1.98); the launches traced: 180 us -> 351 us
  blocking collectives: 91.1 us -> 262 us
    psum x1 -> x2, blocking collectives: 91.1 us -> 262 us  [the longest x1 246 us: by_each_axis(): middle = lax.psum(value, inner_axis)]
where the time goes in v1:
time: 358 us; the launch traced here: 351 us
  blocking collectives  262 us (73%)
  starting transfers between devices  49.4 us (14%)
  other arithmetic  21.6 us (6%)
  waiting for transfers between devices  9.98 us (3%)
  local copies, waits for them, and re-layouts  4.53 us (1%)
    psum x1, blocking collectives, by_each_axis(): middle = lax.psum(value, inner_axis)  246 us
    ppermute x8, starting transfers between devices, extended(): lax.ppermute(lax.slice_in_dim(block, block.shape[dim] - width, None, axis...  32.4 us
    ppermute x8, starting transfers between devices, extended(): lax.ppermute(lax.slice_in_dim(block, 0, width, axis=dim), axis, backward)  17.1 us
    psum x1, blocking collectives, by_each_axis(): return lax.psum(middle, outer_axis)  15.2 us
  transfers between devices with their start and end apart: 16, of which 9 were waited for; matrix products, arithmetic and copies ran while one was open for 1% of the time, Pallas kernels for 0%

profile of v1, /device:TPU:1, one launch (start us, length us, event | category | flops | bytes accessed | tf_op | source)
XLA Modules:
  0.0 350.9 jit_solution(17225364352123133400)
XLA Ops:
  1.4 5.1 %collective-permute-start.1 = (f32[2,3,128]{2,1,0:T(4,128)S(1)}, f32[2,3,128]{2,1,0:T(4,128)S(1)}, u32[]{:S(2)}, u32[]{:S(2)}) collective-permute-start(f32[2,3,128]{2,1,0:T(4,128)S(1)} %get-tuple-element.49), channel_id=1, source_target_pairs={{4,0},{8,4},{12,8},{16,12},{20,16},{24,20},{28,24},{32,28},{36,32}... | collective-permute-start | bytes 9224 | tf_op jit(solution)/shard_map/ppermute | solution.py:20
  6.5 1.9 collective-permute-start
  8.4 1.6 copy.15
  11.7 4.0 %collective-permute-start.2 = (f32[2,14,3]{2,1,0:T(8,128)S(1)}, f32[2,14,3]{2,1,0:T(8,128)S(1)}, u32[]{:S(2)}, u32[]{:S(2)}) collective-permute-start(f32[2,14,3]{2,1,0:T(8,128)S(1)} %get-tuple-element.46), channel_id=1, source_target_pairs={{0,1},{1,2},{2,3},{4,5},{5,6},{6,7},{8,9},{9,10},{10,11},{12,13},{... | collective-permute-start | bytes 1016 | tf_op jit(solution)/shard_map/ppermute | solution.py:17
  15.7 3.0 collective-permute-start.5
  18.7 2.6 collective-permute-start.4
  21.4 1.3 collective-permute-done.5
  23.9 1.3 collective-permute-start.7
  25.2 4.0 %collective-permute-start.6 = (f32[3,64,10,1]{1,3,2,0:T(1,128)S(1)}, f32[3,64,10,1]{1,3,2,0:T(1,128)S(1)}, u32[]{:S(2)}, u32[]{:S(2)}) collective-permute-start(f32[3,64,10,1]{1,3,2,0:T(1,128)S(1)} %get-tuple-element.36), channel_id=1, source_target_pairs={{0,1},{1,2},{2,3},{4,5},{5,6},{6,7},{8,9},{9,10},{10,11},{12,13},{... | collective-permute-start | bytes 23048 | tf_op jit(solution)/shard_map/ppermute | solution.py:17
  32.1 1.9 collective-permute-start.9
  34.1 5.5 %collective-permute-start.8 = (f32[3,64,1,128]{1,3,2,0:T(8,128)S(1)}, f32[3,64,1,128]{1,3,2,0:T(8,128)S(1)}, u32[]{:S(2)}, u32[]{:S(2)}) collective-permute-start(f32[3,64,1,128]{1,3,2,0:T(8,128)S(1)} %get-tuple-element.40), channel_id=1, source_target_pairs={{0,4},{4,8},{8,12},{12,16},{16,20},{20,24},{24,28},{28,32},{32,36}... | collective-permute-start | bytes 294920 | tf_op jit(solution)/shard_map/ppermute | solution.py:17
  39.6 1.4 collective-permute-done.9
  43.5 4.5 %collective-permute-start.10 = (f32[3,64,10,1]{1,3,2,0:T(1,128)S(1)}, f32[3,64,10,1]{1,3,2,0:T(1,128)S(1)}, u32[]{:S(2)}, u32[]{:S(2)}) collective-permute-start(f32[3,64,10,1]{1,3,2,0:T(1,128)S(1)} %get-tuple-element.34), channel_id=1, source_target_pairs={{0,1},{1,2},{2,3},{4,5},{5,6},{6,7},{8,9},{9,10},{10,11},{12,13},{... | collective-permute-start | bytes 23048 | tf_op jit(solution)/shard_map/ppermute | solution.py:17
  51.4 1.9 collective-permute-start.13
  53.3 5.2 %collective-permute-start.12 = (f32[3,64,1,128]{1,3,2,0:T(8,128)S(1)}, f32[3,64,1,128]{1,3,2,0:T(8,128)S(1)}, u32[]{:S(2)}, u32[]{:S(2)}) collective-permute-start(f32[3,64,1,128]{1,3,2,0:T(8,128)S(1)} %get-tuple-element.38), channel_id=1, source_target_pairs={{0,4},{4,8},{8,12},{12,16},{16,20},{20,24},{24,28},{28,32},{32,36}... | collective-permute-start | bytes 294920 | tf_op jit(solution)/shard_map/ppermute | solution.py:17
  58.6 1.4 collective-permute-done.13
  62.5 4.5 %collective-permute-start.14 = (f32[3,64,10,1]{1,3,2,0:T(1,128)S(1)}, f32[3,64,10,1]{1,3,2,0:T(1,128)S(1)}, u32[]{:S(2)}, u32[]{:S(2)}) collective-permute-start(f32[3,64,10,1]{1,3,2,0:T(1,128)S(1)} %get-tuple-element.32), channel_id=1, source_target_pairs={{0,1},{1,2},{2,3},{4,5},{5,6},{6,7},{8,9},{9,10},{10,11},{12,13},{... | collective-permute-start | bytes 23048 | tf_op jit(solution)/shard_map/ppermute | solution.py:17
  69.5 1.7 fusion.77
  73.0 246.4 %all-reduce = (f32[64,64]{1,0:T(8,128)S(1)}, f32[64]{0:T(128)S(1)}) all-reduce(f32[64,64]{1,0:T(8,128)S(1)} %fusion.83, f32[64]{0:T(128)S(1)} %convolution_bitcast_fusion.2), channel_id=1, replica_groups=mesh['gx'=64,'gy'=4] {'gx'}, use_global_device_ids=true, to_apply=%region_2.3 | all-reduce | flops 4160 | bytes 33280 | tf_op jit(solution)/shard_map/psum | solution.py:8
  319.4 15.2 %all-reduce.1 = (f32[64,64]{1,0:T(8,128)S(1)}, f32[64]{0:T(128)S(1)}) all-reduce(f32[64,64]{1,0:T(8,128)S(1)} %get-tuple-element.5, f32[64]{0:T(128)S(1)} %get-tuple-element.6), channel_id=1, replica_groups=mesh['gx'=64,'gy'=4] {'gy'}, use_global_device_ids=true, to_apply=%region_3.4 | all-reduce | flops 4160 | bytes 33280 | tf_op jit(solution)/shard_map/psum | solution.py:9
  334.8 5.8 %cholesky.18 = f32[64,64]{1,0:T(8,128)S(1)} custom-call(f32[64,64]{1,0:T(8,128)S(1)} %fusion.74), custom_call_target="Cholesky" | custom-call | tf_op jit(solution)/shard_map/jit(cholesky)/cholesky | solution.py:93
  342.0 4.9 %custom-call.10 = f32[1,64,64]{1,2,0:T(8,128)S(1)} custom-call(f32[1,64,64]{2,1,0:T(8,128)S(1)} %fusion.70), custom_call_target="InvertDiagBlocksLowerTriangular" | custom-call | tf_op jit(solution)/shard_map/triangular_solve | solution.py:59
  347.5 2.1 fusion.15
  349.6 1.3 copy.19
  (74 shorter events, 21.6 us)
Async XLA Ops:
  1.4 8.9 %collective-permute-start.1 = (f32[2,3,128]{2,1,0:T(4,128)S(1)}, f32[2,3,128]{2,1,0:T(4,128)S(1)}, u32[]{:S(2)}, u32[]{:S(2)}) collective-permute-start(f32[2,3,128]{2,1,0:T(4,128)S(1)} %get-tuple-element.49), channel_id=1, source_target_pairs={{4,0},{8,4},{12,8},{16,12},{20,16},{24,20},{28,24},{32,28},{36,32}... | collective-permute-start | bytes 9224 | tf_op jit(solution)/shard_map/ppermute | solution.py:20
  6.5 3.8 %collective-permute-start = (f32[2,3,128]{2,1,0:T(4,128)S(1)}, f32[2,3,128]{2,1,0:T(4,128)S(1)}, u32[]{:S(2)}, u32[]{:S(2)}) collective-permute-start(f32[2,3,128]{2,1,0:T(4,128)S(1)} %get-tuple-element.48), channel_id=1, source_target_pairs={{0,4},{4,8},{8,12},{12,16},{16,20},{20,24},{24,28},{28,32},{32,36}... | collective-permute-start | bytes 9224 | tf_op jit(solution)/shard_map/ppermute | solution.py:17
  10.4 10.9 %collective-permute-start.3 = (f32[2,14,3]{2,1,0:T(8,128)S(1)}, f32[2,14,3]{2,1,0:T(8,128)S(1)}, u32[]{:S(2)}, u32[]{:S(2)}) collective-permute-start(f32[2,14,3]{2,1,0:T(8,128)S(1)} %get-tuple-element.47), channel_id=1, source_target_pairs={{1,0},{2,1},{3,2},{5,4},{6,5},{7,6},{9,8},{10,9},{11,10},{13,12},{... | collective-permute-start | bytes 1016 | tf_op jit(solution)/shard_map/ppermute | solution.py:20
  11.7 9.6 %collective-permute-start.2 = (f32[2,14,3]{2,1,0:T(8,128)S(1)}, f32[2,14,3]{2,1,0:T(8,128)S(1)}, u32[]{:S(2)}, u32[]{:S(2)}) collective-permute-start(f32[2,14,3]{2,1,0:T(8,128)S(1)} %get-tuple-element.46), channel_id=1, source_target_pairs={{0,1},{1,2},{2,3},{4,5},{5,6},{6,7},{8,9},{9,10},{10,11},{12,13},{... | collective-permute-start | bytes 1016 | tf_op jit(solution)/shard_map/ppermute | solution.py:17
  15.7 7.0 %collective-permute-start.5 = (f32[3,64,1,128]{1,3,2,0:T(8,128)S(1)}, f32[3,64,1,128]{1,3,2,0:T(8,128)S(1)}, u32[]{:S(2)}, u32[]{:S(2)}) collective-permute-start(f32[3,64,1,128]{1,3,2,0:T(8,128)S(1)} %get-tuple-element.43), channel_id=1, source_target_pairs={{4,0},{8,4},{12,8},{16,12},{20,16},{24,20},{28,24},{32,28},{36,32}... | collective-permute-start | bytes 294920 | tf_op jit(solution)/shard_map/ppermute | solution.py:20
  18.7 5.2 %collective-permute-start.4 = (f32[3,64,1,128]{1,3,2,0:T(8,128)S(1)}, f32[3,64,1,128]{1,3,2,0:T(8,128)S(1)}, u32[]{:S(2)}, u32[]{:S(2)}) collective-permute-start(f32[3,64,1,128]{1,3,2,0:T(8,128)S(1)} %get-tuple-element.42), channel_id=1, source_target_pairs={{0,4},{4,8},{8,12},{12,16},{16,20},{20,24},{24,28},{28,32},{32,36}... | collective-permute-start | bytes 294920 | tf_op jit(solution)/shard_map/ppermute | solution.py:17
  23.9 5.5 %collective-permute-start.7 = (f32[3,64,10,1]{1,3,2,0:T(1,128)S(1)}, f32[3,64,10,1]{1,3,2,0:T(1,128)S(1)}, u32[]{:S(2)}, u32[]{:S(2)}) collective-permute-start(f32[3,64,10,1]{1,3,2,0:T(1,128)S(1)} %get-tuple-element.37), channel_id=1, source_target_pairs={{1,0},{2,1},{3,2},{5,4},{6,5},{7,6},{9,8},{10,9},{11,10},{13,12},{... | collective-permute-start | bytes 23048 | tf_op jit(solution)/shard_map/ppermute | solution.py:20
  25.2 4.8 %collective-permute-start.6 = (f32[3,64,10,1]{1,3,2,0:T(1,128)S(1)}, f32[3,64,10,1]{1,3,2,0:T(1,128)S(1)}, u32[]{:S(2)}, u32[]{:S(2)}) collective-permute-start(f32[3,64,10,1]{1,3,2,0:T(1,128)S(1)} %get-tuple-element.36), channel_id=1, source_target_pairs={{0,1},{1,2},{2,3},{4,5},{5,6},{6,7},{8,9},{9,10},{10,11},{12,13},{... | collective-permute-start | bytes 23048 | tf_op jit(solution)/shard_map/ppermute | solution.py:17
  32.1 16.0 %copy-start = (s32[1,1,256]{2,1,0:T(1,128)S(1)}, s32[1,1,256]{2,1,0:T(1,128)}, u32[]{:S(2)}) copy-start(s32[1,1,256]{2,1,0:T(1,128)} %param.9) | copy-start | bytes 3076
  32.1 8.9 %collective-permute-start.9 = (f32[3,64,1,128]{1,3,2,0:T(8,128)S(1)}, f32[3,64,1,128]{1,3,2,0:T(8,128)S(1)}, u32[]{:S(2)}, u32[]{:S(2)}) collective-permute-start(f32[3,64,1,128]{1,3,2,0:T(8,128)S(1)} %get-tuple-element.41), channel_id=1, source_target_pairs={{4,0},{8,4},{12,8},{16,12},{20,16},{24,20},{28,24},{32,28},{36,32}... | collective-permute-start | bytes 294920 | tf_op jit(solution)/shard_map/ppermute | solution.py:20
  34.1 8.1 %collective-permute-start.8 = (f32[3,64,1,128]{1,3,2,0:T(8,128)S(1)}, f32[3,64,1,128]{1,3,2,0:T(8,128)S(1)}, u32[]{:S(2)}, u32[]{:S(2)}) collective-permute-start(f32[3,64,1,128]{1,3,2,0:T(8,128)S(1)} %get-tuple-element.40), channel_id=1, source_target_pairs={{0,4},{4,8},{8,12},{12,16},{16,20},{20,24},{24,28},{28,32},{32,36}... | collective-permute-start | bytes 294920 | tf_op jit(solution)/shard_map/ppermute | solution.py:17
  42.2 5.9 %collective-permute-start.11 = (f32[3,64,10,1]{1,3,2,0:T(1,128)S(1)}, f32[3,64,10,1]{1,3,2,0:T(1,128)S(1)}, u32[]{:S(2)}, u32[]{:S(2)}) collective-permute-start(f32[3,64,10,1]{1,3,2,0:T(1,128)S(1)} %get-tuple-element.35), channel_id=1, source_target_pairs={{1,0},{2,1},{3,2},{5,4},{6,5},{7,6},{9,8},{10,9},{11,10},{13,12},{... | collective-permute-start | bytes 23048 | tf_op jit(solution)/shard_map/ppermute | solution.py:20
  43.5 5.4 %collective-permute-start.10 = (f32[3,64,10,1]{1,3,2,0:T(1,128)S(1)}, f32[3,64,10,1]{1,3,2,0:T(1,128)S(1)}, u32[]{:S(2)}, u32[]{:S(2)}) collective-permute-start(f32[3,64,10,1]{1,3,2,0:T(1,128)S(1)} %get-tuple-element.34), channel_id=1, source_target_pairs={{0,1},{1,2},{2,3},{4,5},{5,6},{6,7},{8,9},{9,10},{10,11},{12,13},{... | collective-permute-start | bytes 23048 | tf_op jit(solution)/shard_map/ppermute | solution.py:17
  51.4 8.6 %collective-permute-start.13 = (f32[3,64,1,128]{1,3,2,0:T(8,128)S(1)}, f32[3,64,1,128]{1,3,2,0:T(8,128)S(1)}, u32[]{:S(2)}, u32[]{:S(2)}) collective-permute-start(f32[3,64,1,128]{1,3,2,0:T(8,128)S(1)} %get-tuple-element.39), channel_id=1, source_target_pairs={{4,0},{8,4},{12,8},{16,12},{20,16},{24,20},{28,24},{32,28},{36,32}... | collective-permute-start | bytes 294920 | tf_op jit(solution)/shard_map/ppermute | solution.py:20
  53.3 7.8 %collective-permute-start.12 = (f32[3,64,1,128]{1,3,2,0:T(8,128)S(1)}, f32[3,64,1,128]{1,3,2,0:T(8,128)S(1)}, u32[]{:S(2)}, u32[]{:S(2)}) collective-permute-start(f32[3,64,1,128]{1,3,2,0:T(8,128)S(1)} %get-tuple-element.38), channel_id=1, source_target_pairs={{0,4},{4,8},{8,12},{12,16},{16,20},{20,24},{24,28},{28,32},{32,36}... | collective-permute-start | bytes 294920 | tf_op jit(solution)/shard_map/ppermute | solution.py:17
  61.2 5.9 %collective-permute-start.15 = (f32[3,64,10,1]{1,3,2,0:T(1,128)S(1)}, f32[3,64,10,1]{1,3,2,0:T(1,128)S(1)}, u32[]{:S(2)}, u32[]{:S(2)}) collective-permute-start(f32[3,64,10,1]{1,3,2,0:T(1,128)S(1)} %get-tuple-element.33), channel_id=1, source_target_pairs={{1,0},{2,1},{3,2},{5,4},{6,5},{7,6},{9,8},{10,9},{11,10},{13,12},{... | collective-permute-start | bytes 23048 | tf_op jit(solution)/shard_map/ppermute | solution.py:20
  62.5 5.4 %collective-permute-start.14 = (f32[3,64,10,1]{1,3,2,0:T(1,128)S(1)}, f32[3,64,10,1]{1,3,2,0:T(1,128)S(1)}, u32[]{:S(2)}, u32[]{:S(2)}) collective-permute-start(f32[3,64,10,1]{1,3,2,0:T(1,128)S(1)} %get-tuple-element.32), channel_id=1, source_target_pairs={{0,1},{1,2},{2,3},{4,5},{5,6},{6,7},{8,9},{9,10},{10,11},{12,13},{... | collective-permute-start | bytes 23048 | tf_op jit(solution)/shard_map/ppermute | solution.py:17
  71.3 1.0 copy-start.1
  71.3 1.0 copy-start.2
